TPU v7x, 512 devices: a whole 4x8x8 slice. The times are simulated.
512 devices in a mesh: freq: 8 (over z_hi, core), tile: 64 (over y, z_lo, x).
Axes of the slice: x: 4, y: 8, z: 8 (z_hi: 4, z_lo: 2; z = z_hi * 2 + z_lo), core: 2. Of those that a mesh axis runs over, the one named last changes fastest.
Arguments:
- spectra: bfloat16 [2, 128, 256, 8192], P(None, None, 'freq', 'tile'), may hold values from -450 to 450
- seg_mask: int32 [128, 8192], P(None, 'tile'), may hold values 0 or 1
Outputs:
- coherence: bfloat16 [64, 2, 256, 128, 128], P('tile', None, None, 'freq')
All inputs are finite; a program needn't handle non-finite values. No bound on the sum of `seg_mask` on one device may be relied on, other than what follows from the above.
Results may differ from a plain program's by a relative error of at most 0.012.
The roundings to bfloat16 on the way count: a program that leaves them out, or rounds other values in their place, can miss the bound.
Values may be sent and summed in bfloat16 or wider, within the bound.
A program may use at most 64 MiB of HBM per device.

v0:
```python
import math

import jax
import jax.numpy as jnp
from jax import lax
from jax.sharding import PartitionSpec as P

F = 256
LAGS = 512


WATER = 0.05


def passed_along(block, axis, distance):
    devices = range(lax.axis_size(axis))
    route = [((i - distance) % len(devices), i) for i in devices]
    return lax.ppermute(block, axis, route)


def dft_tables(lag_count, freq_count):
    lag_index = jnp.arange(lag_count, dtype=jnp.int32)[:, None]
    freq_index = jnp.arange(freq_count, dtype=jnp.int32)[None, :]
    phase = (lag_index * freq_index % lag_count).astype(jnp.float32) * (2.0 * math.pi / lag_count)
    return (jnp.cos(phase).astype(jnp.bfloat16), jnp.sin(phase).astype(jnp.bfloat16))


def shards(spectra, seg_mask):
    tile_count = lax.axis_size("tile")
    half_axis = tile_count // 2
    freq_count = lax.axis_size("freq")
    seg_count = spectra.shape[1]
    band_size = spectra.shape[2]
    block_size = spectra.shape[3]
    group_rows = block_size // freq_count
    masked = spectra * seg_mask.astype(jnp.bfloat16)[None, :, None, :]
    partner = passed_along(masked, "tile", half_axis)
    own_power = jnp.sum(jnp.square(masked.astype(jnp.float32)), axis=(0, 1)) / seg_count + 1e-05
    own_rows = masked.reshape(2 * seg_count, band_size, block_size)
    partner_cols = jnp.concatenate(
        [
            jnp.concatenate([partner[0], partner[1]], axis=0),
            jnp.concatenate([partner[1], -partner[0]], axis=0),
        ],
        axis=2,
    )
    cross_spec = (
        jnp.einsum("sfa,sfc->fac", own_rows, partner_cols, preferred_element_type=jnp.float32)
        / seg_count
    )
    far_power = jnp.sum(jnp.square(partner.astype(jnp.float32)), axis=(0, 1)) / seg_count + 1e-05
    own_total, far_total = lax.psum(
        (jnp.sum(own_power, axis=0), jnp.sum(far_power, axis=0)), "freq"
    )
    own_weight = own_power + WATER * (own_total / F)[None, :]
    far_weight = far_power + WATER * (far_total / F)[None, :]
    own_spec = (cross_spec / own_weight[:, :, None]).astype(jnp.bfloat16)
    far_spec = (cross_spec / jnp.concatenate([far_weight, far_weight], axis=1)[:, None, :]).astype(
        jnp.bfloat16
    )
    mirror_re = far_spec[:, :, :block_size].astype(jnp.float32)
    mirror_im = far_spec[:, :, block_size:].astype(jnp.float32)
    sym_re = 0.5 * (own_spec[:, :, :block_size].astype(jnp.float32) + mirror_re)
    sym_im = 0.5 * (own_spec[:, :, block_size:].astype(jnp.float32) + mirror_im)
    symmetric = jnp.concatenate([sym_re, sym_im], axis=2).astype(jnp.bfloat16)
    symmetric = symmetric.reshape(band_size, freq_count, group_rows, 2 * block_size)
    cos_tab, sin_tab = dft_tables(LAGS, F)
    lag_table = jnp.concatenate([cos_tab, sin_tab], axis=1)
    out_table = jnp.concatenate([cos_tab.T, -sin_tab.T], axis=0)
    norm_scale = 1.0 / math.sqrt(LAGS)
    received = lax.all_to_all(symmetric, "freq", split_axis=1, concat_axis=0, tiled=True)
    row_count = received.shape[2]
    col_count = row_count * block_size
    unpacked = received.reshape(F, row_count, 2, block_size)
    real_part = unpacked[:, :, 0, :].reshape(F, col_count)
    imag_part = unpacked[:, :, 1, :].reshape(F, col_count)
    stacked = jnp.concatenate(
        [
            jnp.concatenate([real_part, -imag_part], axis=0),
            jnp.concatenate([imag_part, real_part], axis=0),
        ],
        axis=1,
    )
    lag_vals = jnp.dot(lag_table, stacked, preferred_element_type=jnp.float32)
    lag_re = lag_vals[:, :col_count]
    lag_im = lag_vals[:, col_count:]
    energy = lag_re * lag_re + lag_im * lag_im
    mean_energy = jnp.mean(energy, axis=0, keepdims=True)
    phase_part = (lag_re / jnp.sqrt(energy + 0.25 * mean_energy + 1e-05)).astype(jnp.bfloat16)
    spectrum = jnp.dot(out_table, phase_part, preferred_element_type=jnp.float32) * norm_scale
    regrouped = spectrum.astype(jnp.bfloat16).reshape(2, F, row_count, block_size)
    return regrouped[None]


def solution(mesh):
    placed = (P(None, None, "freq", "tile"), P(None, "tile"))
    return jax.shard_map(
        shards,
        mesh=mesh,
        in_specs=placed,
        out_specs=P("tile", None, None, "freq", None),
        check_vma=False,
    )
```

profile of v0, /device:TPU:16, one launch (start us, length us, event | category | flops | bytes accessed | tf_op | source)
XLA Modules:
  0.0 218.0 jit_solution(5361067966086408391)
XLA Ops:
  0.0 0.8 convert_element_type.64
  0.8 2.5 %multiply_reduce_fusion.1 = (f32[32,128]{1,0:T(8,128)S(1)}, bf16[2,128,32,128]{3,1,2,0:T(8,128)(2,1)S(1)}) fusion(bf16[128,128]{1,0:T(8,128)(2,1)S(1)} %convert_element_type.64, bf16[2,128,32,128]{3,2,1,0:T(8,128)(2,1)} %param.2), kind=kLoop, calls=%fused_computation.23 | loop fusion | flops 4190208 | bytes 4243456 | tf_op jit(solution)/shard_map/reduce_sum | solution.py:38
  3.4 5.9 %collective-permute-start = (bf16[2,128,32,128]{3,1,2,0:T(8,128)(2,1)S(1)}, bf16[2,128,32,128]{3,1,2,0:T(8,128)(2,1)S(1)}, u32[]{:S(2)}, u32[]{:S(2)}) collective-permute-start(bf16[2,128,32,128]{3,1,2,0:T(8,128)(2,1)S(1)} %get-tuple-element.8), channel_id=1, source_target_pairs={{32,0},{33,1},{34,2},{35,3},{36,4},{37,5},{38,6},{39,7},{40,8},{41... | collective-permute-start | bytes 6291464 | tf_op jit(solution)/shard_map/ppermute | solution.py:18
  9.3 2.7 %copy.5 = bf16[2,128,32,128]{3,2,1,0:T(8,128)(2,1)} copy(bf16[2,128,32,128]{3,1,2,0:T(8,128)(2,1)S(1)} %get-tuple-element.8) | data formatting | bytes 4194304 | tf_op jit(solution)/shard_map/mul | solution.py:36
  12.0 89.9 %collective-permute-done = bf16[2,128,32,128]{3,1,2,0:T(8,128)(2,1)S(1)} collective-permute-done((bf16[2,128,32,128]{3,1,2,0:T(8,128)(2,1)S(1)}, bf16[2,128,32,128]{3,1,2,0:T(8,128)(2,1)S(1)}, u32[]{:S(2)}, u32[]{:S(2)}) %collective-permute-start) | collective-permute-done | bytes 2097184 | tf_op jit(solution)/shard_map/ppermute | solution.py:18
  101.9 0.5 multiply_reduce_fusion
  102.4 22.7 %all-reduce = (f32[128]{0:T(128)S(1)}, f32[128]{0:T(128)S(1)}) all-reduce(f32[128]{0:T(128)S(1)} %fusion.45, f32[128]{0:T(128)S(1)} %fusion.43), channel_id=1, replica_groups=mesh['freq'=8,'tile'=64] {'freq'}, use_global_device_ids=true, to_apply=%region_5.0 | all-reduce | flops 256 | bytes 2048 | tf_op jit(solution)/shard_map/psum | solution.py:52
  125.1 0.0 copy-start.2
  125.2 0.2 slice_bitcast_fusion.1
  125.4 0.1 fusion.50
  125.6 1.2 copy-done.2
  126.7 3.3 %divide_convert_fusion.1 = (bf16[32,128,256]{2,1,0:T(8,128)(2,1)S(1)}, bf16[32,128,256]{2,1,0:T(8,128)(2,1)S(1)}) fusion(f32[32,128]{1,0:T(8,128)S(1)} %fusion.42, f32[32,256]{1,0:T(8,128)S(1)} %pad_maximum_fusion.1, bf16[128,32,128]{2,0,1:T(8,128)(2,1)S(1)} %fusion.50, bf16[128,32,128]{2,0,1:T(8,128)(2,1)S(1)} %get-tuple-element.16, ...), kind=kOutput, calls=%fused_computation.22 | convolution fusion | flops 558891008 | bytes 9486336 | tf_op jit(solution)/shard_map/sfa,sfc->fac/dot_general | solution.py:48
  130.0 0.7 multiply_convert_fusion.4
  130.8 0.3 pad_maximum_fusion
  131.1 1.5 copy.11
  132.6 3.8 %all-to-all-start = ((bf16[32,8,16,256]{3,2,0,1:T(8,128)(2,1)}), bf16[32,8,16,256]{3,2,0,1:T(8,128)(2,1)S(1)}, u32[]{:S(2)}, u32[]{:S(2)}) async-start(bf16[32,8,16,256]{3,2,0,1:T(8,128)(2,1)} %copy.11), calls=%async_computation | async-start | bytes 4194304 | tf_op jit(solution)/shard_map/all_to_all | solution.py:71
  136.4 2.0 cosine_convert_fusion.1
  138.4 2.6 %fusion.41 = bf16[256,512]{1,0:T(8,128)(2,1)} fusion(), kind=kLoop, calls=%fused_computation.63 | loop fusion | flops 2359296 | bytes 262144 | tf_op jit(solution)/shard_map/neg | solution.py:69
  141.0 2.9 %sine_convert_fusion = (bf16[512,256]{1,0:T(8,128)(2,1)}, bf16[512,256]{1,0:T(8,128)(2,1)}) fusion(), kind=kLoop, calls=%fused_computation.53 | loop fusion | flops 2097152 | bytes 524288 | tf_op jit(solution)/shard_map/convert_element_type | solution.py:25
  143.9 44.2 %all-to-all-done = bf16[32,8,16,256]{3,2,0,1:T(8,128)(2,1)S(1)} async-done(((bf16[32,8,16,256]{3,2,0,1:T(8,128)(2,1)}), bf16[32,8,16,256]{3,2,0,1:T(8,128)(2,1)S(1)}, u32[]{:S(2)}, u32[]{:S(2)}) %all-to-all-start) | async-done | bytes 2097184 | tf_op jit(solution)/shard_map/all_to_all | solution.py:71
  188.2 0.0 copy-start
  188.2 1.3 copy-done
  189.5 2.5 %reshape.38 = bf16[256,16,2,128]{3,2,1,0:T(2,128)(2,1)S(1)} reshape(bf16[8,32,1,16,256]{4,3,1,0,2:T(8,128)(2,1)} %bitcast.23) | data formatting | bytes 4194304 | tf_op jit(solution)/shard_map/reshape | solution.py:74
  192.0 4.2 %fusion.51 = (bf16[256,16,1,128]{3,2,1,0:T(2,128)(2,1)}, bf16[256,16,1,128]{3,2,1,0:T(2,128)(2,1)}) fusion(bf16[256,16,2,128]{3,2,1,0:T(2,128)(2,1)S(1)} %reshape.38), kind=kLoop, calls=%fused_computation.80 | loop fusion | bytes 4194304 | tf_op jit(solution)/shard_map/slice | solution.py:76
  196.2 0.0 copy-start.1
  196.2 4.7 %copy.10 = bf16[256,16,1,128]{0,3,1,2:T(8,128)(2,1)S(1)} copy(bf16[256,16,1,128]{3,2,1,0:T(2,128)(2,1)} %get-tuple-element.13) | data formatting | bytes 2097152 | tf_op jit(solution)/shard_map/slice | solution.py:76
  200.9 1.1 bitcast_negate_fusion
  202.0 0.0 copy-done.1
  202.0 3.7 %copy.9 = bf16[256,16,1,128]{0,3,1,2:T(8,128)(2,1)} copy(bf16[256,16,1,128]{3,2,1,0:T(2,128)(2,1)S(1)} %copy-done.1) | data formatting | bytes 2097152 | tf_op jit(solution)/shard_map/slice | solution.py:75
  205.7 7.6 %fusion.9 = f32[512,4096]{1,0:T(8,128)S(1)} fusion(bf16[256,2048]{0,1:T(8,128)(2,1)} %bitcast.28, bf16[256,2048]{0,1:T(8,128)(2,1)S(1)} %bitcast.24, bf16[256,2048]{0,1:T(8,128)(2,1)} %bitcast_negate_fusion, bf16[512,256]{1,0:T(8,128)(2,1)} %get-tuple-element.19, bf16[512,256]{1,0:T(8,128)(2,1)} %get-tuple-element.20), kind=kOutput, calls=%fused_computation.10 | convolution fusion | flops 2165309440 | bytes 12058624 | tf_op jit(solution)/shard_map/dot_general | solution.py:84
  213.3 0.0 copy-start.3
  213.3 0.8 fusion.22
  214.1 0.2 copy-done.3
  214.2 1.8 fusion.20
  216.1 2.0 copy.12
  (7 shorter events, 0.1 us)
Async XLA Ops:
  3.4 98.6 %collective-permute-start = (bf16[2,128,32,128]{3,1,2,0:T(8,128)(2,1)S(1)}, bf16[2,128,32,128]{3,1,2,0:T(8,128)(2,1)S(1)}, u32[]{:S(2)}, u32[]{:S(2)}) collective-permute-start(bf16[2,128,32,128]{3,1,2,0:T(8,128)(2,1)S(1)} %get-tuple-element.8), channel_id=1, source_target_pairs={{32,0},{33,1},{34,2},{35,3},{36,4},{37,5},{38,6},{39,7},{40,8},{41... | collective-permute-start | bytes 6291464 | tf_op jit(solution)/shard_map/ppermute | solution.py:18
  125.1 1.6 copy-start.2
  132.6 55.6 %all-to-all-start = ((bf16[32,8,16,256]{3,2,0,1:T(8,128)(2,1)}), bf16[32,8,16,256]{3,2,0,1:T(8,128)(2,1)S(1)}, u32[]{:S(2)}, u32[]{:S(2)}) async-start(bf16[32,8,16,256]{3,2,0,1:T(8,128)(2,1)} %copy.11), calls=%async_computation | async-start | bytes 4194304 | tf_op jit(solution)/shard_map/all_to_all | solution.py:71
  188.2 1.3 copy-start
  196.2 5.8 %copy-start.1 = (bf16[256,16,1,128]{3,2,1,0:T(2,128)(2,1)S(1)}, bf16[256,16,1,128]{3,2,1,0:T(2,128)(2,1)}, u32[]{:S(2)}) copy-start(bf16[256,16,1,128]{3,2,1,0:T(2,128)(2,1)} %get-tuple-element.14) | copy-start | bytes 3145732
  213.3 1.0 copy-start.3
where the time goes:
time: 219 us; the launch traced here: 218 us
  waiting for transfers between devices  134 us (61%)
  local copies, waits for them, and re-layouts  24.1 us (11%)
  blocking collectives  22.7 us (10%)
  other arithmetic  14.5 us (7%)
  matrix products  12.7 us (6%)
  starting transfers between devices  9.72 us (4%)
    ppermute x1, waiting for transfers between devices, passed_along(): return lax.ppermute(block, axis, route)  89.9 us
    all_to_all x1, waiting for transfers between devices, shards(): lax.all_to_all(symmetric, 'freq', split_axis=1, concat_axis=0, tiled=True)  44.2 us
    psum x1, blocking collectives, shards(): lax.psum((jnp.sum(own_power, axis=0), jnp.sum(far_power, axis=0)), 'freq')  22.7 us
    slice x2, local copies, waits for them, and re-layouts, shards(): imag_part = unpacked[:, :, 1, :].reshape(F, col_count)  8.82 us
    dot_general x1, matrix products, shards(): lag_vals = jnp.dot(lag_table, stacked, preferred_element_type=jnp.float32)  7.57 us
    ppermute x1, starting transfers between devices, passed_along(): return lax.ppermute(block, axis, route)  5.94 us
    unnamed x9, local copies, waits for them, and re-layouts  4.6 us
  transfers between devices with their start and end apart: 2, of which 2 were waited for; matrix products, arithmetic and copies ran while one was open for 5% of the time, Pallas kernels for 0%

commit v1 on v0

v1 whole, which is shorter than its diff:
```python
import math

import jax
import jax.numpy as jnp
import numpy as np
from jax import lax
from jax.experimental import pallas as pl
from jax.experimental.pallas import tpu as pltpu
from jax.sharding import PartitionSpec as P

F = 256
LAGS = 512
WATER = 0.05
STEP = 2
MESH = pl.DeviceIdType.MESH


def dft_tables(band, groups):
    lag = np.arange(LAGS)[:, None]

    def pair(freq):
        phase = (lag * freq[None, :] % LAGS).astype(np.float32) * np.float32(2.0 * math.pi / LAGS)
        return np.cos(phase.astype(np.float64)), np.sin(phase.astype(np.float64))

    chunk, src, step = np.meshgrid(
        np.arange(band // STEP), np.arange(groups), np.arange(STEP), indexing="ij"
    )
    cos_in, sin_in = pair((src * band + chunk * STEP + step).reshape(-1))
    real_rows = np.stack([cos_in, -sin_in], axis=2).reshape(LAGS, 2 * F)
    imag_rows = np.stack([sin_in, cos_in], axis=2).reshape(LAGS, 2 * F)
    cos_out, sin_out = pair(np.arange(F))
    lag_table = np.concatenate([real_rows, imag_rows], axis=0)
    out_table = np.concatenate([cos_out.T, -sin_out.T], axis=0)
    return jnp.asarray(lag_table, jnp.bfloat16), jnp.asarray(out_table, jnp.bfloat16)


def kernel(
    x_ref, mask_ref, lag_tab, out_tab, o_ref,
    wide, sent, lhs, far, sym, got, flip, rhs, spec, power, totals, inv_own, inv_far, inv_col,
    y_send, y_recv, w_sem, t_send, t_recv, z_send, z_recv,
):
    groups = lax.axis_size("freq")
    tiles = lax.axis_size("tile")
    me = lax.axis_index("freq")
    partner = {"tile": lax.rem(lax.axis_index("tile") + tiles // 2, tiles)}
    peers = [lax.rem(me + d, groups) for d in range(1, groups)]
    segs, band, block = x_ref.shape[1:]
    rows = block // groups
    chunks = band // STEP
    depth = 2 * STEP * groups

    barrier = pltpu.get_barrier_semaphore()
    for dev in [partner] + [{"freq": q} for q in peers]:
        pl.semaphore_signal(barrier, inc=1, device_id=dev, device_id_type=MESH)

    def y_copy(c):
        return pltpu.make_async_remote_copy(
            src_ref=sent.at[pl.ds(c * STEP, STEP)],
            dst_ref=far.at[pl.ds(c * STEP, STEP)],
            send_sem=y_send.at[c],
            recv_sem=y_recv.at[c],
            device_id=partner,
            device_id_type=MESH,
        )

    def z_copy(c, d):
        return pltpu.make_async_remote_copy(
            src_ref=sym.at[peers[d], pl.ds(c * STEP, STEP)],
            dst_ref=got.at[me, pl.ds(c * STEP, STEP)],
            send_sem=z_send.at[c, d],
            recv_sem=z_recv.at[c, d],
            device_id={"freq": peers[d]},
            device_id_type=MESH,
        )

    def t_copy(d):
        return pltpu.make_async_remote_copy(
            src_ref=totals.at[me],
            dst_ref=totals.at[me],
            send_sem=t_send.at[d],
            recv_sem=t_recv.at[d],
            device_id={"freq": peers[d]},
            device_id_type=MESH,
        )

    w_copy = pltpu.make_async_remote_copy(
        src_ref=inv_own,
        dst_ref=inv_far,
        send_sem=w_sem.at[0],
        recv_sem=w_sem.at[1],
        device_id=partner,
        device_id_type=MESH,
    )

    per = 8

    @pl.loop(0, segs // per)
    def _(i):
        for part in range(2):
            vals = x_ref[part, pl.ds(i * per, per)].astype(jnp.float32)
            start = pl.multiple_of((part * segs + i * per) * band, per * band)
            wide[pl.ds(start, per * band), :] = vals.reshape(per * band, block)

    mask = mask_ref[...].astype(jnp.float32)
    both = jnp.concatenate([mask, mask], axis=0)

    @pl.loop(0, band)
    def _(f):
        vals = wide[pl.ds(f, 2 * segs, stride=band), :] * both
        power[pl.ds(f, 1), :] = jnp.sum(vals * vals, axis=0, keepdims=True) / segs + 1e-05
        sent[f] = vals.astype(jnp.bfloat16)

    total = jnp.sum(power[...], axis=0, keepdims=True)
    totals[me] = jnp.broadcast_to(total, (8, block))
    pl.semaphore_wait(barrier, groups)
    for d in range(groups - 1):
        t_copy(d).start()
    for c in range(2):
        y_copy(c).start()

    @pl.loop(0, band)
    def _(f):
        turned = sent[f].astype(jnp.float32).T
        real, imag = turned[:, :segs], turned[:, segs:]
        lhs[f, :block] = turned.astype(jnp.bfloat16)
        lhs[f, block:] = jnp.concatenate([-imag, real], axis=1).astype(jnp.bfloat16)

    for d in range(groups - 1):
        t_copy(d).wait()
    whole = totals[0]
    for g in range(1, groups):
        whole = whole + totals[g]
    inv_own[...] = (1.0 / segs) / (power[...] + WATER * (whole[:1] / F))
    w_copy.start()

    @pl.loop(2, chunks)
    def _(c):
        y_copy(c).start()

    @pl.loop(0, band)
    def _(f):
        inv_col[f] = jnp.broadcast_to(inv_own[pl.ds(f, 1), :], (block, block)).T

    w_copy.wait()

    def land(c):
        for d in range(groups - 1):
            z_copy(c, d).wait()
        part = got[:, pl.ds(c * STEP, STEP)].astype(jnp.float32)
        flip[...] = part.reshape(depth * rows, block)
        for r in range(rows):
            at = pl.multiple_of(c * depth, depth)
            rhs[r, pl.ds(at, depth), :] = flip[pl.ds(r, depth, stride=rows), :].astype(jnp.bfloat16)

    def step(c):
        y_copy(c).wait()
        for i in range(STEP):
            f = c * STEP + i
            cross = jnp.dot(lhs[f], far[f], preferred_element_type=jnp.float32)
            row = inv_far[pl.ds(f, 1), :]
            col = inv_col[f]
            for part in range(2):
                vals = cross[part * block : (part + 1) * block]
                decon = (vals * col).astype(jnp.bfloat16).astype(jnp.float32)
                mirror = (vals * row).astype(jnp.bfloat16).astype(jnp.float32)
                both_sides = (0.5 * (decon + mirror)).astype(jnp.bfloat16)
                sym[:, f, part] = both_sides.reshape(groups, rows, block)
            got[me, f] = sym[me, f]
        for d in range(groups - 1):
            z_copy(c, d).start()

    lag = 2
    for c in range(lag):
        step(c)

    @pl.loop(lag, chunks)
    def _(c):
        step(c)
        land(c - lag)

    for c in range(chunks - lag, chunks):
        land(c)

    norm = 1.0 / math.sqrt(LAGS)

    @pl.loop(0, rows // 2)
    def _(i):
        pair = jnp.concatenate([rhs[2 * i], rhs[2 * i + 1]], axis=1)
        lags = jnp.dot(lag_tab[...], pair, preferred_element_type=jnp.float32)
        real, imag = lags[:LAGS], lags[LAGS:]
        energy = real * real + imag * imag
        mean = jnp.sum(energy, axis=0, keepdims=True) / LAGS
        phase = (real * lax.rsqrt(energy + (0.25 * mean + 1e-05))).astype(jnp.bfloat16)
        out = jnp.dot(out_tab[...], phase, preferred_element_type=jnp.float32) * norm
        for half in range(2):
            spec[pl.ds(2 * i + half, 2 * F, stride=rows), :] = out[:, half * block : (half + 1) * block]

    blk = 16

    @pl.loop(0, F // blk)
    def _(k):
        for part in range(2):
            at = pl.multiple_of((part * F + k * blk) * rows, blk * rows)
            vals = spec[pl.ds(at, blk * rows), :].astype(jnp.bfloat16)
            o_ref[part, pl.ds(k * blk, blk)] = vals.reshape(blk, rows, block)


def shards(spectra, seg_mask):
    groups = lax.axis_size("freq")
    _, segs, band, block = spectra.shape
    rows = block // groups
    chunks = band // STEP
    depth = 2 * STEP * groups
    lag_tab, out_tab = dft_tables(band, groups)
    vmem = pl.BlockSpec(memory_space=pltpu.VMEM)
    bf16, f32 = jnp.bfloat16, jnp.float32
    out = pl.pallas_call(
        kernel,
        out_shape=jax.ShapeDtypeStruct((2, F, rows, block), bf16),
        in_specs=[vmem] * 4,
        out_specs=vmem,
        scratch_shapes=[
            pltpu.VMEM((2 * segs * band, block), f32),
            pltpu.VMEM((band, 2 * segs, block), bf16),
            pltpu.VMEM((band, 2 * block, 2 * segs), bf16),
            pltpu.VMEM((band, 2 * segs, block), bf16),
            pltpu.VMEM((groups, band, 2, rows, block), bf16),
            pltpu.VMEM((groups, band, 2, rows, block), bf16),
            pltpu.VMEM((depth * rows, block), f32),
            pltpu.VMEM((rows, 2 * F, block), bf16),
            pltpu.VMEM((2 * F * rows, block), f32),
            pltpu.VMEM((band, block), f32),
            pltpu.VMEM((groups, 8, block), f32),
            pltpu.VMEM((band, block), f32),
            pltpu.VMEM((band, block), f32),
            pltpu.VMEM((band, block, block), f32),
            pltpu.SemaphoreType.DMA((chunks,)),
            pltpu.SemaphoreType.DMA((chunks,)),
            pltpu.SemaphoreType.DMA((2,)),
            pltpu.SemaphoreType.DMA((groups - 1,)),
            pltpu.SemaphoreType.DMA((groups - 1,)),
            pltpu.SemaphoreType.DMA((chunks, groups - 1)),
            pltpu.SemaphoreType.DMA((chunks, groups - 1)),
        ],
        compiler_params=pltpu.CompilerParams(
            collective_id=0, has_side_effects=True, vmem_limit_bytes=56 * 1024 * 1024
        ),
        name="interferometry",
    )(spectra, seg_mask, lag_tab, out_tab)
    return out[None]


def solution(mesh):
    placed = (P(None, None, "freq", "tile"), P(None, "tile"))
    return jax.shard_map(
        shards,
        mesh=mesh,
        in_specs=placed,
        out_specs=P("tile", None, None, "freq", None),
        check_vma=False,
    )
```

time: 219 us -> 135 us (0.62)
  the two profiles are of different devices: /device:TPU:16 before, /device:TPU:1 now
where the time goes in v1:
time: 135 us
  Pallas kernels  132 us (98%)
  local copies, waits for them, and re-layouts  3.27 us (2%)
    pallas_call x1, Pallas kernels, shards(): pl.pallas_call(kernel, out_shape=jax.ShapeDtypeStruct((2, F, rows, block)...  132 us
    unnamed x1, local copies, waits for them, and re-layouts  3.27 us

profile of v1, /device:TPU:1, one launch (start us, length us, event | category | flops | bytes accessed | tf_op | source)
XLA Modules:
  0.0 135.1 jit_solution(13375081476989682825)
XLA Ops:
  0.0 131.8 %interferometry.1 = bf16[2,256,16,128]{3,2,1,0:T(8,128)(2,1)} custom-call(bf16[2,128,32,128]{3,2,1,0:T(8,128)(2,1)} %x_ref.1, s32[128,128]{1,0:T(8,128)} %mask_ref.1, bf16[1024,512]{1,0:T(8,128)(2,1)} %constant.4.clone.lag_tab, bf16[512,512]{1,0:T(8,128)(2,1)} %constant.5.clone.out_tab), custom_call_target="tpu_custom_call" | custom-call | tf_op jit(solution)/shard_map/interferometry/pallas_call | solution.py:217
  131.8 3.3 %copy.6 = bf16[1,2,256,16,128]{4,3,2,1,0:T(8,128)(2,1)} copy(bf16[1,2,256,16,128]{4,3,2,1,0:T(8,128)(2,1)} %bitcast.1) | data formatting | bytes 4194304

commit v2 on v1

v2 whole, which is shorter than its diff:
```python
import contextlib
import math

import jax
import jax.numpy as jnp
import numpy as np
from jax import lax
from jax.experimental import pallas as pl
from jax.experimental.pallas import tpu as pltpu
from jax.sharding import PartitionSpec as P

F = 256
LAGS = 512
HALF = LAGS // 2
WATER = 0.05
STEP = 2
AHEAD = 6
FIRST = 2
MESH = pl.DeviceIdType.MESH


def scope(name):
    return contextlib.nullcontext()


def dft_tables(band, groups):
    def pair(lag, freq):
        phase = (lag[:, None] * freq[None, :] % LAGS) * (2.0 * math.pi / LAGS)
        return np.cos(phase), np.sin(phase)

    chunk, src, step = np.meshgrid(
        np.arange(band // STEP), np.arange(groups), np.arange(STEP), indexing="ij"
    )
    order = (src * band + chunk * STEP + step).reshape(-1)
    cos_in, sin_in = pair(np.arange(HALF), order)
    sin_in[0] = pair(np.array([HALF]), order)[0][0]
    cos_out, sin_out = pair(np.arange(HALF), np.arange(F))
    lag_table = np.concatenate([cos_in, sin_in], axis=0)
    out_table = np.concatenate([cos_out.T, -sin_out.T], axis=0)
    return jnp.asarray(lag_table, jnp.bfloat16), jnp.asarray(out_table, jnp.bfloat16)


def kernel(
    x_hbm, mask_ref, lag_hbm, tab_hbm, o_ref,
    x_ref, lag_tab, out_tab, wide, sent, lhs, far, sym, got, flip, rhs, spec,
    power, totals, inv_own, inv_far, inv_col,
    in_sem, y_send, y_recv, w_sem, t_sem, z_send, z_recv, credit,
):
    groups = lax.axis_size("freq")
    tiles = lax.axis_size("tile")
    me = lax.axis_index("freq")
    partner = {"tile": lax.rem(lax.axis_index("tile") + tiles // 2, tiles)}
    ahead = {"tile": lax.rem(lax.axis_index("tile") + tiles // 4, tiles)}
    behind = {"tile": lax.rem(lax.axis_index("tile") + tiles - tiles // 4, tiles)}
    peers = [lax.rem(me + d, groups) for d in range(1, groups)]
    segs, band, block = x_ref.shape[1:]
    rows = block // groups
    chunks = band // STEP
    depth = STEP * groups

    barrier = pltpu.get_barrier_semaphore()
    for dev in [partner, ahead, behind] + [{"freq": q} for q in peers]:
        pl.semaphore_signal(barrier, inc=1, device_id=dev, device_id_type=MESH)

    def x_copy(part):
        return pltpu.make_async_copy(x_hbm.at[part], x_ref.at[part], in_sem.at[part])

    tab_copies = [
        pltpu.make_async_copy(lag_hbm, lag_tab, in_sem.at[2]),
        pltpu.make_async_copy(tab_hbm, out_tab, in_sem.at[3]),
    ]
    for part in range(2):
        x_copy(part).start()

    def y_copy(c):
        return pltpu.make_async_remote_copy(
            src_ref=sent.at[pl.ds(c * STEP, STEP)],
            dst_ref=far.at[pl.ds(c * STEP, STEP)],
            send_sem=y_send,
            recv_sem=y_recv.at[c],
            device_id=partner,
            device_id_type=MESH,
        )

    def z_copy(c, d):
        return pltpu.make_async_remote_copy(
            src_ref=sym.at[peers[d], pl.ds(c * STEP, STEP)],
            dst_ref=got.at[me, pl.ds(c * STEP, STEP)],
            send_sem=z_send,
            recv_sem=z_recv.at[c],
            device_id={"freq": peers[d]},
            device_id_type=MESH,
        )

    def t_copy(d):
        return pltpu.make_async_remote_copy(
            src_ref=totals.at[me],
            dst_ref=totals.at[me],
            send_sem=t_sem.at[0],
            recv_sem=t_sem.at[1],
            device_id={"freq": peers[d]},
            device_id_type=MESH,
        )

    def wait_bytes(ref, sem):
        pltpu.make_async_copy(ref, ref, sem).wait()

    w_copy = pltpu.make_async_remote_copy(
        src_ref=inv_own,
        dst_ref=inv_far,
        send_sem=w_sem.at[0],
        recv_sem=w_sem.at[1],
        device_id=partner,
        device_id_type=MESH,
    )

    pitch = band + 1
    per = 8
    with scope("A_convert"):
        for part in range(2):
            x_copy(part).wait()

            @pl.loop(0, segs // per)
            def _(i):
                vals = x_ref[part, pl.ds(i * per, per)].astype(jnp.float32)
                for k in range(per):
                    wide[pl.ds((part * segs + i * per + k) * pitch, band), :] = vals[k]

    for copy in tab_copies:
        copy.start()

    def lay_out(f):
        total = jnp.zeros((8, block), jnp.float32)
        for h in range(2 * segs // 16):
            vals = wide[pl.ds(f + h * 16 * pitch, 16, stride=pitch), :]
            at = h * 16 % segs
            vals = vals * mask_ref[at : at + 16].astype(jnp.float32)
            sent[f, h * 16 : (h + 1) * 16] = vals.astype(jnp.bfloat16)
            square = vals * vals
            total = total + (square[:8] + square[8:])
        power[pl.ds(f, 1), :] = jnp.sum(total, axis=0, keepdims=True) / segs + 1e-05

    with scope("B_first"):

        @pl.loop(0, FIRST * STEP)
        def _(f):
            lay_out(f)

    with scope("C_barrier"):
        pl.semaphore_wait(barrier, groups + 2)
    for c in range(FIRST):
        y_copy(c).start()

    with scope("B_rest"):

        @pl.loop(FIRST * STEP, band)
        def _(f):
            lay_out(f)

    total = jnp.sum(power[...], axis=0, keepdims=True)
    totals[me] = jnp.broadcast_to(total, (8, block))
    for d in range(groups - 1):
        t_copy(d).start()

    with scope("D_lhs"):

        @pl.loop(0, band)
        def _(f):
            turned = sent[f].astype(jnp.float32).T
            real, imag = turned[:, :segs], turned[:, segs:]
            lhs[f, :block] = turned.astype(jnp.bfloat16)
            lhs[f, block:] = jnp.concatenate([-imag, real], axis=1).astype(jnp.bfloat16)

    with scope("E_twait"):
        wait_bytes(totals.at[pl.ds(0, groups - 1)], t_sem.at[1])
        wait_bytes(totals.at[pl.ds(0, groups - 1)], t_sem.at[0])
    whole = totals[0]
    for g in range(1, groups):
        whole = whole + totals[g]
    inv_own[...] = (1.0 / segs) / (power[...] + WATER * (whole[:1] / F))
    w_copy.start()
    for c in range(FIRST, AHEAD):
        y_copy(c).start()

    @pl.loop(0, band)
    def _(f):
        inv_col[f] = jnp.broadcast_to(inv_own[pl.ds(f, 1), :], (block, block)).T

    def take(c, more):
        y_copy(c).wait_recv()
        if more:
            pl.semaphore_signal(credit, inc=1, device_id=ahead, device_id_type=MESH)
            pl.semaphore_wait(credit, 1)
            y_copy(c + AHEAD).start()

    for c in range(FIRST):
        with scope("F_take"):
            take(c, True)

    with scope("F_wwait"):
        w_copy.wait_recv()

    def land(c):
        wait_bytes(got.at[pl.ds(0, groups - 1), pl.ds(0, STEP)], z_recv.at[c])
        for src in range(groups):
            for i in range(STEP):
                for part in range(2):
                    at = (part * depth + src * STEP + i) * (rows + 1)
                    flip[at : at + rows, :] = got[src, c * STEP + i, part].astype(jnp.float32)
        for r in range(rows):
            for part in range(2):
                at = pl.multiple_of(c * depth, depth)
                vals = flip[pl.ds(part * depth * (rows + 1) + r, depth, stride=rows + 1), :]
                rhs[r, part, pl.ds(at, depth), :] = vals.astype(jnp.bfloat16)

    def step(c):
        for i in range(STEP):
            f = c * STEP + i
            cross = jnp.dot(lhs[f], far[f], preferred_element_type=jnp.float32)
            row = inv_far[pl.ds(f, 1), :]
            col = inv_col[f]
            for part in range(2):
                vals = cross[part * block : (part + 1) * block]
                decon = (vals * col).astype(jnp.bfloat16).astype(jnp.float32)
                mirror = (vals * row).astype(jnp.bfloat16).astype(jnp.float32)
                both_sides = (0.5 * (decon + mirror)).astype(jnp.bfloat16)
                sym[:, f, part] = both_sides.reshape(groups, rows, block)
            got[me, f] = sym[me, f]
        for d in range(groups - 1):
            z_copy(c, d).start()

    lag = 2
    for c in range(lag):
        with scope("G_step"):
            step(c)

    @pl.loop(lag, chunks - AHEAD)
    def _(c):
        with scope("H_take"):
            take(c, True)
        with scope("H_step"):
            step(c)
        with scope("I_land"):
            land(c - lag)

    @pl.loop(chunks - AHEAD, chunks)
    def _(c):
        with scope("H_take"):
            take(c, False)
        with scope("H_step"):
            step(c)
        with scope("I_land"):
            land(c - lag)

    for copy in tab_copies:
        copy.wait()
    for c in range(chunks - lag, chunks):
        with scope("J_land"):
            land(c)

    norm = 1.0 / math.sqrt(LAGS)
    first = lax.broadcasted_iota(jnp.int32, (8, block), 0) == 0
    odd = lax.rem(lax.broadcasted_iota(jnp.int32, (8, block), 0), 2) == 1

    def with_row0(general, special):
        return jnp.concatenate([jnp.where(first, special[:8], general[:8]), general[8:]], axis=0)

    def both_lags(r):
        pair = jnp.concatenate([rhs[r, 0], rhs[r, 1]], axis=1)
        prod = jnp.dot(lag_tab[...], pair, preferred_element_type=jnp.float32)
        cos_re, cos_im = prod[:HALF, :block], prod[:HALF, block:]
        sin_re, sin_im = prod[HALF:, :block], prod[HALF:, block:]
        up_re = with_row0(cos_re - sin_im, cos_re)
        up_im = with_row0(cos_im + sin_re, cos_im)
        down_re = with_row0(cos_re + sin_im, sin_re)
        down_im = with_row0(cos_im - sin_re, sin_im)
        up = up_re * up_re + up_im * up_im
        down = down_re * down_re + down_im * down_im
        mean = jnp.sum(up + down, axis=0, keepdims=True) / LAGS
        base = 0.25 * mean + 1e-05
        up_norm = up_re * lax.rsqrt(up + base)
        down_norm = down_re * lax.rsqrt(down + base)
        middle = down_norm[:1]
        even = with_row0(up_norm + down_norm, up_norm).astype(jnp.bfloat16)
        return even, (up_norm - down_norm).astype(jnp.bfloat16), middle

    with scope("K_transform"):

        @pl.loop(0, rows // 2)
        def _(i):
            even0, odd0, mid0 = both_lags(2 * i)
            even1, odd1, mid1 = both_lags(2 * i + 1)
            even = jnp.concatenate([even0, even1], axis=1)
            odds = jnp.concatenate([odd0, odd1], axis=1)
            re = jnp.dot(out_tab[:F], even, preferred_element_type=jnp.float32)
            im = jnp.dot(out_tab[F:], odds, preferred_element_type=jnp.float32)
            for half, mid in ((0, mid0), (1, mid1)):
                cols = slice(half * block, (half + 1) * block)
                signed = jnp.where(odd, -mid, mid)
                signed = jnp.broadcast_to(signed[None], (F // 8, 8, block)).reshape(F, block)
                at = (2 * i + half) * (2 * F + 1)
                spec[pl.ds(at, F), :] = (re[:, cols] + signed) * norm
                spec[pl.ds(at + F, F), :] = im[:, cols] * norm

    blk = 8
    with scope("L_conv"):

        @pl.loop(0, F // blk)
        def _(k):
            for part in range(2):
                for i in range(blk):
                    at = part * F + k * blk + i
                    vals = spec[pl.ds(at, rows, stride=2 * F + 1), :]
                    o_ref[part, k * blk + i] = vals.astype(jnp.bfloat16)

    with scope("M_drain"):
        w_copy.wait_send()
        wait_bytes(sent, y_send)
        wait_bytes(sym.at[pl.ds(0, groups - 1)], z_send)


def shards(spectra, seg_mask):
    groups = lax.axis_size("freq")
    _, segs, band, block = spectra.shape
    rows = block // groups
    chunks = band // STEP
    depth = STEP * groups
    lag_tab, out_tab = dft_tables(band, groups)
    vmem = pl.BlockSpec(memory_space=pltpu.VMEM)
    hbm = pl.BlockSpec(memory_space=pltpu.HBM)
    bf16, f32 = jnp.bfloat16, jnp.float32
    out = pl.pallas_call(
        kernel,
        out_shape=jax.ShapeDtypeStruct((2, F, rows, block), bf16),
        in_specs=[hbm, vmem, hbm, hbm],
        out_specs=vmem,
        scratch_shapes=[
            pltpu.VMEM(spectra.shape, bf16),
            pltpu.VMEM(lag_tab.shape, bf16),
            pltpu.VMEM(out_tab.shape, bf16),
            pltpu.VMEM((2 * segs * (band + 1), block), f32),
            pltpu.VMEM((band, 2 * segs, block), bf16),
            pltpu.VMEM((band, 2 * block, 2 * segs), bf16),
            pltpu.VMEM((band, 2 * segs, block), bf16),
            pltpu.VMEM((groups, band, 2, rows, block), bf16),
            pltpu.VMEM((groups, band, 2, rows, block), bf16),
            pltpu.VMEM((2 * depth * (rows + 1), block), f32),
            pltpu.VMEM((rows, 2, F, block), bf16),
            pltpu.VMEM((rows * (2 * F + 1) + 8, block), f32),
            pltpu.VMEM((band, block), f32),
            pltpu.VMEM((groups, 8, block), f32),
            pltpu.VMEM((band, block), f32),
            pltpu.VMEM((band, block), f32),
            pltpu.VMEM((band, block, block), f32),
            pltpu.SemaphoreType.DMA((4,)),
            pltpu.SemaphoreType.DMA,
            pltpu.SemaphoreType.DMA((chunks,)),
            pltpu.SemaphoreType.DMA((2,)),
            pltpu.SemaphoreType.DMA((2,)),
            pltpu.SemaphoreType.DMA,
            pltpu.SemaphoreType.DMA((chunks,)),
            pltpu.SemaphoreType.REGULAR,
        ],
        compiler_params=pltpu.CompilerParams(
            collective_id=0, has_side_effects=True, vmem_limit_bytes=40 * 1024 * 1024
        ),
        name="interferometry",
    )(*(pltpu.with_memory_space_constraint(a, pltpu.HBM) for a in (spectra, seg_mask, lag_tab, out_tab)))
    return out[None]


def solution(mesh):
    placed = (P(None, None, "freq", "tile"), P(None, "tile"))
    return jax.shard_map(
        shards,
        mesh=mesh,
        in_specs=placed,
        out_specs=P("tile", None, None, "freq", None),
        check_vma=False,
    )
```

time: 135 us -> 123 us (0.911)
  Pallas kernels: 132 us -> 121 us
  local copies, waits for them, and re-layouts: 3.27 us -> 1.32 us
    pallas_call x1, Pallas kernels: 132 us -> 121 us  [shards(): pl.pallas_call(kernel, out_shape=jax.ShapeDtypeStruct((2, F, rows, block)...]
    unnamed x1, local copies, waits for them, and re-layouts: 3.27 us -> 1.32 us
where the time goes in v2:
time: 123 us; the launch traced here: 122 us
  Pallas kernels  121 us (98%)
  local copies, waits for them, and re-layouts  1.32 us (1%)
    pallas_call x1, Pallas kernels, shards(): pl.pallas_call(kernel, out_shape=jax.ShapeDtypeStruct((2, F, rows, block)...  121 us

profile of v2, /device:TPU:1, one launch (start us, length us, event | category | flops | bytes accessed | tf_op | source)
XLA Modules:
  0.0 122.2 jit_solution(14808034352010451576)
XLA Ops:
  0.0 120.9 %interferometry.1 = bf16[2,256,16,128]{3,2,1,0:T(8,128)(2,1)S(1)} custom-call(bf16[2,128,32,128]{3,2,1,0:T(8,128)(2,1)} %x_hbm.1, s32[128,128]{1,0:T(8,128)} %mask_ref.1, bf16[512,256]{1,0:T(8,128)(2,1)} %constant.4.clone.lag_hbm, bf16[512,256]{1,0:T(8,128)(2,1)} %constant.5.clone.tab_hbm), custom_call_target="tpu_custom_call" | custom-call | tf_op jit(solution)/shard_map/interferometry/pallas_call | solution.py:332
  120.9 1.3 %copy.6 = bf16[1,2,256,16,128]{4,3,2,1,0:T(8,128)(2,1)} copy(bf16[1,2,256,16,128]{4,3,2,1,0:T(8,128)(2,1)S(1)} %bitcast.1) | data formatting | bytes 4194304

commit v3 on v2

--- a/solution.py
+++ b/solution.py
@@ -14,7 +14,8 @@
 HALF = LAGS // 2
 WATER = 0.05
 STEP = 2
-AHEAD = 6
+AHEAD = 4
+BEHIND = 5
 FIRST = 2
 MESH = pl.DeviceIdType.MESH
 
@@ -41,9 +42,9 @@
 
 
 def kernel(
-    x_hbm, mask_ref, lag_hbm, tab_hbm, o_ref,
-    x_ref, lag_tab, out_tab, wide, sent, lhs, far, sym, got, flip, rhs, spec,
-    power, totals, inv_own, inv_far, inv_col,
+    x_hbm, mask_hbm, lag_hbm, tab_hbm, o_ref,
+    x_ref, mask_ref, lag_tab, out_tab, wide, sent, lhs, far, sym, got, flip, rhs, spec,
+    prod0, prod1, prod2, prod3, power, totals, own_total, far_total, inv_own, inv_col,
     in_sem, y_send, y_recv, w_sem, t_sem, z_send, z_recv, credit,
 ):
     groups = lax.axis_size("freq")
@@ -58,10 +59,6 @@
     chunks = band // STEP
     depth = STEP * groups
 
-    barrier = pltpu.get_barrier_semaphore()
-    for dev in [partner, ahead, behind] + [{"freq": q} for q in peers]:
-        pl.semaphore_signal(barrier, inc=1, device_id=dev, device_id_type=MESH)
-
     def x_copy(part):
         return pltpu.make_async_copy(x_hbm.at[part], x_ref.at[part], in_sem.at[part])
 
@@ -69,28 +66,38 @@
         pltpu.make_async_copy(lag_hbm, lag_tab, in_sem.at[2]),
         pltpu.make_async_copy(tab_hbm, out_tab, in_sem.at[3]),
     ]
+    mask_copy = pltpu.make_async_copy(mask_hbm, mask_ref, in_sem.at[4])
+
+    barrier = pltpu.get_barrier_semaphore()
     for part in range(2):
         x_copy(part).start()
-
-    def y_copy(c):
+    mask_copy.start()
+    for dev in [partner, ahead, behind] + [{"freq": q} for q in peers]:
+        pl.semaphore_signal(barrier, inc=1, device_id=dev, device_id_type=MESH)
+
+    def y_copy(c, first=None, count=STEP):
+        part = pl.ds(c * STEP if first is None else first, count)
         return pltpu.make_async_remote_copy(
-            src_ref=sent.at[pl.ds(c * STEP, STEP)],
-            dst_ref=far.at[pl.ds(c * STEP, STEP)],
+            src_ref=sent.at[part],
+            dst_ref=far.at[part],
             send_sem=y_send,
             recv_sem=y_recv.at[c],
             device_id=partner,
             device_id_type=MESH,
         )
 
-    def z_copy(c, d):
+    def z_copy(c, d, first=None, count=STEP):
+        part = pl.ds(c * STEP if first is None else first, count)
         return pltpu.make_async_remote_copy(
-            src_ref=sym.at[peers[d], pl.ds(c * STEP, STEP)],
-            dst_ref=got.at[me, pl.ds(c * STEP, STEP)],
+            src_ref=sym.at[peers[d], part],
+            dst_ref=got.at[me, part],
             send_sem=z_send,
             recv_sem=z_recv.at[c],
             device_id={"freq": peers[d]},
             device_id_type=MESH,
         )
+
+    last = [(chunks - 1 + i, band - STEP + i, 1) for i in range(STEP)]
 
     def t_copy(d):
         return pltpu.make_async_remote_copy(
@@ -106,8 +113,8 @@
         pltpu.make_async_copy(ref, ref, sem).wait()
 
     w_copy = pltpu.make_async_remote_copy(
-        src_ref=inv_own,
-        dst_ref=inv_far,
+        src_ref=own_total,
+        dst_ref=far_total,
         send_sem=w_sem.at[0],
         recv_sem=w_sem.at[1],
         device_id=partner,
@@ -128,17 +135,23 @@
 
     for copy in tab_copies:
         copy.start()
+    mask_copy.wait()
+
+    def mean_square(vals):
+        squares = [v * v for v in vals]
+        while len(squares) > 1:
+            squares = [a + b for a, b in zip(squares[::2], squares[1::2])]
+        return jnp.sum(squares[0], axis=0, keepdims=True) / segs + 1e-05
 
     def lay_out(f):
-        total = jnp.zeros((8, block), jnp.float32)
+        parts = []
         for h in range(2 * segs // 16):
             vals = wide[pl.ds(f + h * 16 * pitch, 16, stride=pitch), :]
             at = h * 16 % segs
             vals = vals * mask_ref[at : at + 16].astype(jnp.float32)
             sent[f, h * 16 : (h + 1) * 16] = vals.astype(jnp.bfloat16)
-            square = vals * vals
-            total = total + (square[:8] + square[8:])
-        power[pl.ds(f, 1), :] = jnp.sum(total, axis=0, keepdims=True) / segs + 1e-05
+            parts += [vals[:8], vals[8:]]
+        power[pl.ds(f, 1), :] = mean_square(parts)
 
     with scope("B_first"):
 
@@ -177,31 +190,44 @@
     whole = totals[0]
     for g in range(1, groups):
         whole = whole + totals[g]
-    inv_own[...] = (1.0 / segs) / (power[...] + WATER * (whole[:1] / F))
+    own_total[...] = whole
     w_copy.start()
     for c in range(FIRST, AHEAD):
         y_copy(c).start()
 
+    def inverse(power_row, total_row):
+        return (1.0 / segs) / (power_row + WATER * (total_row / F))
+
+    inv_own[...] = inverse(power[...], own_total[:1])
+
     @pl.loop(0, band)
     def _(f):
         inv_col[f] = jnp.broadcast_to(inv_own[pl.ds(f, 1), :], (block, block)).T
 
-    def take(c, more):
+    def take(c, more=True):
         y_copy(c).wait_recv()
         if more:
             pl.semaphore_signal(credit, inc=1, device_id=ahead, device_id_type=MESH)
             pl.semaphore_wait(credit, 1)
-            y_copy(c + AHEAD).start()
+            if isinstance(c, int) and c + AHEAD == chunks - 1:
+                for piece in last:
+                    y_copy(*piece).start()
+            else:
+                y_copy(c + AHEAD).start()
 
     for c in range(FIRST):
         with scope("F_take"):
-            take(c, True)
+            take(c)
 
     with scope("F_wwait"):
         w_copy.wait_recv()
 
     def land(c):
-        wait_bytes(got.at[pl.ds(0, groups - 1), pl.ds(0, STEP)], z_recv.at[c])
+        if isinstance(c, int) and c == chunks - 1:
+            for sem, _, count in last:
+                wait_bytes(got.at[pl.ds(0, groups - 1), pl.ds(0, count)], z_recv.at[sem])
+        else:
+            wait_bytes(got.at[pl.ds(0, groups - 1), pl.ds(0, STEP)], z_recv.at[c])
         for src in range(groups):
             for i in range(STEP):
                 for part in range(2):
@@ -213,51 +239,74 @@
                 vals = flip[pl.ds(part * depth * (rows + 1) + r, depth, stride=rows + 1), :]
                 rhs[r, part, pl.ds(at, depth), :] = vals.astype(jnp.bfloat16)
 
+    def symmetric(f):
+        cross = jnp.dot(lhs[f], far[f], preferred_element_type=jnp.float32)
+        vals = far[f].astype(jnp.float32)
+        row = inverse(mean_square([vals[k : k + 8] for k in range(0, 2 * segs, 8)]), far_total[:1])
+        col = inv_col[f]
+        for part in range(2):
+            vals = cross[part * block : (part + 1) * block]
+            decon = (vals * col).astype(jnp.bfloat16).astype(jnp.float32)
+            mirror = (vals * row).astype(jnp.bfloat16).astype(jnp.float32)
+            both_sides = (0.5 * (decon + mirror)).astype(jnp.bfloat16)
+            sym[:, f, part] = both_sides.reshape(groups, rows, block)
+        got[me, f] = sym[me, f]
+
     def step(c):
         for i in range(STEP):
-            f = c * STEP + i
-            cross = jnp.dot(lhs[f], far[f], preferred_element_type=jnp.float32)
-            row = inv_far[pl.ds(f, 1), :]
-            col = inv_col[f]
-            for part in range(2):
-                vals = cross[part * block : (part + 1) * block]
-                decon = (vals * col).astype(jnp.bfloat16).astype(jnp.float32)
-                mirror = (vals * row).astype(jnp.bfloat16).astype(jnp.float32)
-                both_sides = (0.5 * (decon + mirror)).astype(jnp.bfloat16)
-                sym[:, f, part] = both_sides.reshape(groups, rows, block)
-            got[me, f] = sym[me, f]
+            symmetric(c * STEP + i)
         for d in range(groups - 1):
             z_copy(c, d).start()
 
-    lag = 2
-    for c in range(lag):
-        with scope("G_step"):
+    with scope("G_step"):
+        for c in range(FIRST):
             step(c)
 
-    @pl.loop(lag, chunks - AHEAD)
-    def _(c):
+    def round_of(c, more):
         with scope("H_take"):
-            take(c, True)
+            take(c, more)
         with scope("H_step"):
             step(c)
+
+    def round_and_land(c, more):
+        round_of(c, more)
         with scope("I_land"):
-            land(c - lag)
-
-    @pl.loop(chunks - AHEAD, chunks)
+            land(c - BEHIND)
+
+    @pl.loop(FIRST, BEHIND)
     def _(c):
+        round_of(c, True)
+
+    @pl.loop(BEHIND, chunks - AHEAD - 1)
+    def _(c):
+        round_and_land(c, True)
+
+    round_and_land(chunks - AHEAD - 1, True)
+
+    @pl.loop(chunks - AHEAD, chunks - 1)
+    def _(c):
+        round_and_land(c, False)
+
+    for sem, f, count in last:
         with scope("H_take"):
-            take(c, False)
+            y_copy(sem, f, count).wait_recv()
         with scope("H_step"):
-            step(c)
-        with scope("I_land"):
-            land(c - lag)
+            symmetric(f)
+            for d in range(groups - 1):
+                z_copy(sem, d, f, count).start()
 
     for copy in tab_copies:
         copy.wait()
-    for c in range(chunks - lag, chunks):
+
+    @pl.loop(chunks - 1 - BEHIND, chunks - 1)
+    def _(c):
         with scope("J_land"):
             land(c)
 
+    with scope("J_last"):
+        land(chunks - 1)
+
+    prod = [prod0, prod1, prod2, prod3]
     norm = 1.0 / math.sqrt(LAGS)
     first = lax.broadcasted_iota(jnp.int32, (8, block), 0) == 0
     odd = lax.rem(lax.broadcasted_iota(jnp.int32, (8, block), 0), 2) == 1
@@ -265,9 +314,11 @@
     def with_row0(general, special):
         return jnp.concatenate([jnp.where(first, special[:8], general[:8]), general[8:]], axis=0)
 
-    def both_lags(r):
+    def products(r, out):
         pair = jnp.concatenate([rhs[r, 0], rhs[r, 1]], axis=1)
-        prod = jnp.dot(lag_tab[...], pair, preferred_element_type=jnp.float32)
+        out[...] = jnp.dot(lag_tab[...], pair, preferred_element_type=jnp.float32)
+
+    def both_lags(prod):
         cos_re, cos_im = prod[:HALF, :block], prod[:HALF, block:]
         sin_re, sin_im = prod[HALF:, :block], prod[HALF:, block:]
         up_re = with_row0(cos_re - sin_im, cos_re)
@@ -286,10 +337,9 @@
 
     with scope("K_transform"):
 
-        @pl.loop(0, rows // 2)
-        def _(i):
-            even0, odd0, mid0 = both_lags(2 * i)
-            even1, odd1, mid1 = both_lags(2 * i + 1)
+        def spectrum(r, prods):
+            even0, odd0, mid0 = both_lags(prods[0])
+            even1, odd1, mid1 = both_lags(prods[1])
             even = jnp.concatenate([even0, even1], axis=1)
             odds = jnp.concatenate([odd0, odd1], axis=1)
             re = jnp.dot(out_tab[:F], even, preferred_element_type=jnp.float32)
@@ -298,9 +348,21 @@
                 cols = slice(half * block, (half + 1) * block)
                 signed = jnp.where(odd, -mid, mid)
                 signed = jnp.broadcast_to(signed[None], (F // 8, 8, block)).reshape(F, block)
-                at = (2 * i + half) * (2 * F + 1)
-                spec[pl.ds(at, F), :] = (re[:, cols] + signed) * norm
-                spec[pl.ds(at + F, F), :] = im[:, cols] * norm
+                at = (r + half) * (2 * F + 1)
+                spec[pl.ds(at, F), :] = re[:, cols] + signed
+                spec[pl.ds(at + F, F), :] = im[:, cols]
+
+        for k in range(2):
+            products(k, prod[k])
+
+        @pl.loop(0, rows // 4)
+        def _(i):
+            for k in range(2):
+                r = 4 * i + 2 * k
+                ready = prod[2 * k : 2 * k + 2]
+                for m in range(2):
+                    products(lax.rem(r + 2 + m, rows), prod[2 - 2 * k + m])
+                spectrum(r, ready)
 
     blk = 8
     with scope("L_conv"):
@@ -311,7 +373,7 @@
                 for i in range(blk):
                     at = part * F + k * blk + i
                     vals = spec[pl.ds(at, rows, stride=2 * F + 1), :]
-                    o_ref[part, k * blk + i] = vals.astype(jnp.bfloat16)
+                    o_ref[part, k * blk + i] = (vals * norm).astype(jnp.bfloat16)
 
     with scope("M_drain"):
         w_copy.wait_send()
@@ -332,10 +394,11 @@
     out = pl.pallas_call(
         kernel,
         out_shape=jax.ShapeDtypeStruct((2, F, rows, block), bf16),
-        in_specs=[hbm, vmem, hbm, hbm],
+        in_specs=[hbm] * 4,
         out_specs=vmem,
         scratch_shapes=[
             pltpu.VMEM(spectra.shape, bf16),
+            pltpu.VMEM(seg_mask.shape, seg_mask.dtype),
             pltpu.VMEM(lag_tab.shape, bf16),
             pltpu.VMEM(out_tab.shape, bf16),
             pltpu.VMEM((2 * segs * (band + 1), block), f32),
@@ -347,18 +410,20 @@
             pltpu.VMEM((2 * depth * (rows + 1), block), f32),
             pltpu.VMEM((rows, 2, F, block), bf16),
             pltpu.VMEM((rows * (2 * F + 1) + 8, block), f32),
+            *[pltpu.VMEM((2 * HALF, 2 * block), f32)] * 4,
             pltpu.VMEM((band, block), f32),
             pltpu.VMEM((groups, 8, block), f32),
-            pltpu.VMEM((band, block), f32),
+            pltpu.VMEM((8, block), f32),
+            pltpu.VMEM((8, block), f32),
             pltpu.VMEM((band, block), f32),
             pltpu.VMEM((band, block, block), f32),
-            pltpu.SemaphoreType.DMA((4,)),
+            pltpu.SemaphoreType.DMA((5,)),
             pltpu.SemaphoreType.DMA,
-            pltpu.SemaphoreType.DMA((chunks,)),
+            pltpu.SemaphoreType.DMA((chunks + STEP - 1,)),
             pltpu.SemaphoreType.DMA((2,)),
             pltpu.SemaphoreType.DMA((2,)),
             pltpu.SemaphoreType.DMA,
-            pltpu.SemaphoreType.DMA((chunks,)),
+            pltpu.SemaphoreType.DMA((chunks + STEP - 1,)),
             pltpu.SemaphoreType.REGULAR,
         ],
         compiler_params=pltpu.CompilerParams(

time: 123 us -> 120 us (0.976)
  Pallas kernels: 121 us -> 118 us
    pallas_call x1, Pallas kernels: 121 us -> 118 us  [shards(): pl.pallas_call(kernel, out_shape=jax.ShapeDtypeStruct((2, F, rows, block)...]
where the time goes in v3:
time: 120 us; the launch traced here: 119 us
  Pallas kernels  118 us (98%)
  local copies, waits for them, and re-layouts  1.32 us (1%)
    pallas_call x1, Pallas kernels, shards(): pl.pallas_call(kernel, out_shape=jax.ShapeDtypeStruct((2, F, rows, block)...  118 us

profile of v3, /device:TPU:1, one launch (start us, length us, event | category | flops | bytes accessed | tf_op | source)
XLA Modules:
  0.0 118.9 jit_solution(7079916466178750238)
XLA Ops:
  0.0 117.6 %interferometry.1 = bf16[2,256,16,128]{3,2,1,0:T(8,128)(2,1)S(1)} custom-call(bf16[2,128,32,128]{3,2,1,0:T(8,128)(2,1)} %x_hbm.1, s32[128,128]{1,0:T(8,128)} %mask_hbm.1, bf16[512,256]{1,0:T(8,128)(2,1)} %constant.4.clone.lag_hbm, bf16[512,256]{1,0:T(8,128)(2,1)} %constant.5.clone.tab_hbm), custom_call_target="tpu_custom_call" | custom-call | tf_op jit(solution)/shard_map/interferometry/pallas_call | solution.py:394
  117.6 1.3 %copy.6 = bf16[1,2,256,16,128]{4,3,2,1,0:T(8,128)(2,1)} copy(bf16[1,2,256,16,128]{4,3,2,1,0:T(8,128)(2,1)S(1)} %bitcast.1) | data formatting | bytes 4194304

commit v4 on v3

--- a/solution.py
+++ b/solution.py
@@ -14,7 +14,8 @@
 HALF = LAGS // 2
 WATER = 0.05
 STEP = 2
-AHEAD = 4
+AHEAD = 5
+TAIL = 5
 BEHIND = 5
 FIRST = 2
 MESH = pl.DeviceIdType.MESH
@@ -44,7 +45,7 @@
 def kernel(
     x_hbm, mask_hbm, lag_hbm, tab_hbm, o_ref,
     x_ref, mask_ref, lag_tab, out_tab, wide, sent, lhs, far, sym, got, flip, rhs, spec,
-    prod0, prod1, prod2, prod3, power, totals, own_total, far_total, inv_own, inv_col,
+    prod0, prod1, prod2, prod3, energy, power, totals, own_total, far_total, inv_own, inv_col,
     in_sem, y_send, y_recv, w_sem, t_sem, z_send, z_recv, credit,
 ):
     groups = lax.axis_size("freq")
@@ -192,6 +193,7 @@
         whole = whole + totals[g]
     own_total[...] = whole
     w_copy.start()
+    energy[...] = jnp.zeros_like(energy)
     for c in range(FIRST, AHEAD):
         y_copy(c).start()
 
@@ -209,11 +211,10 @@
         if more:
             pl.semaphore_signal(credit, inc=1, device_id=ahead, device_id_type=MESH)
             pl.semaphore_wait(credit, 1)
-            if isinstance(c, int) and c + AHEAD == chunks - 1:
-                for piece in last:
-                    y_copy(*piece).start()
+            if more is True:
+                y_copy(c + AHEAD).start()
             else:
-                y_copy(c + AHEAD).start()
+                y_copy(*more).start()
 
     for c in range(FIRST):
         with scope("F_take"):
@@ -228,11 +229,15 @@
                 wait_bytes(got.at[pl.ds(0, groups - 1), pl.ds(0, count)], z_recv.at[sem])
         else:
             wait_bytes(got.at[pl.ds(0, groups - 1), pl.ds(0, STEP)], z_recv.at[c])
+        squares = [jnp.zeros((rows, block), jnp.float32)] * 2
         for src in range(groups):
             for i in range(STEP):
                 for part in range(2):
                     at = (part * depth + src * STEP + i) * (rows + 1)
-                    flip[at : at + rows, :] = got[src, c * STEP + i, part].astype(jnp.float32)
+                    vals = got[src, c * STEP + i, part].astype(jnp.float32)
+                    flip[at : at + rows, :] = vals
+                    squares[part] = squares[part] + vals * vals
+        energy[...] += squares[0] + squares[1]
         for r in range(rows):
             for part in range(2):
                 at = pl.multiple_of(c * depth, depth)
@@ -281,11 +286,9 @@
     def _(c):
         round_and_land(c, True)
 
-    round_and_land(chunks - AHEAD - 1, True)
-
-    @pl.loop(chunks - AHEAD, chunks - 1)
-    def _(c):
-        round_and_land(c, False)
+    hold = dict(zip(range(chunks - TAIL, chunks - TAIL + STEP), last))
+    for c in range(chunks - AHEAD - 1, chunks - 1):
+        round_and_land(c, hold.get(c, False))
 
     for sem, f, count in last:
         with scope("H_take"):
@@ -318,28 +321,33 @@
         pair = jnp.concatenate([rhs[r, 0], rhs[r, 1]], axis=1)
         out[...] = jnp.dot(lag_tab[...], pair, preferred_element_type=jnp.float32)
 
-    def both_lags(prod):
-        cos_re, cos_im = prod[:HALF, :block], prod[:HALF, block:]
-        sin_re, sin_im = prod[HALF:, :block], prod[HALF:, block:]
-        up_re = with_row0(cos_re - sin_im, cos_re)
-        up_im = with_row0(cos_im + sin_re, cos_im)
-        down_re = with_row0(cos_re + sin_im, sin_re)
-        down_im = with_row0(cos_im - sin_re, sin_im)
-        up = up_re * up_re + up_im * up_im
-        down = down_re * down_re + down_im * down_im
-        mean = jnp.sum(up + down, axis=0, keepdims=True) / LAGS
-        base = 0.25 * mean + 1e-05
-        up_norm = up_re * lax.rsqrt(up + base)
-        down_norm = down_re * lax.rsqrt(down + base)
-        middle = down_norm[:1]
-        even = with_row0(up_norm + down_norm, up_norm).astype(jnp.bfloat16)
-        return even, (up_norm - down_norm).astype(jnp.bfloat16), middle
+    def both_lags(r, prod):
+        base = 0.25 * energy[pl.ds(r, 1), :] + 1e-05
+        evens, odds = [], []
+        for b in range(0, HALF, 32):
+            cos_re, cos_im = prod[b : b + 32, :block], prod[b : b + 32, block:]
+            at = HALF + b
+            sin_re, sin_im = prod[at : at + 32, :block], prod[at : at + 32, block:]
+            up_re, up_im = cos_re - sin_im, cos_im + sin_re
+            down_re, down_im = cos_re + sin_im, cos_im - sin_re
+            if b == 0:
+                up_re, up_im = with_row0(up_re, cos_re), with_row0(up_im, cos_im)
+                down_re, down_im = with_row0(down_re, sin_re), with_row0(down_im, sin_im)
+            up_norm = up_re * lax.rsqrt(up_re * up_re + up_im * up_im + base)
+            down_norm = down_re * lax.rsqrt(down_re * down_re + down_im * down_im + base)
+            even = up_norm + down_norm
+            if b == 0:
+                middle = down_norm[:1]
+                even = with_row0(even, up_norm)
+            evens.append(even.astype(jnp.bfloat16))
+            odds.append((up_norm - down_norm).astype(jnp.bfloat16))
+        return jnp.concatenate(evens, axis=0), jnp.concatenate(odds, axis=0), middle
 
     with scope("K_transform"):
 
         def spectrum(r, prods):
-            even0, odd0, mid0 = both_lags(prods[0])
-            even1, odd1, mid1 = both_lags(prods[1])
+            even0, odd0, mid0 = both_lags(r, prods[0])
+            even1, odd1, mid1 = both_lags(r + 1, prods[1])
             even = jnp.concatenate([even0, even1], axis=1)
             odds = jnp.concatenate([odd0, odd1], axis=1)
             re = jnp.dot(out_tab[:F], even, preferred_element_type=jnp.float32)
@@ -411,6 +419,7 @@
             pltpu.VMEM((rows, 2, F, block), bf16),
             pltpu.VMEM((rows * (2 * F + 1) + 8, block), f32),
             *[pltpu.VMEM((2 * HALF, 2 * block), f32)] * 4,
+            pltpu.VMEM((rows, block), f32),
             pltpu.VMEM((band, block), f32),
             pltpu.VMEM((groups, 8, block), f32),
             pltpu.VMEM((8, block), f32),

time: 120 us -> 119 us (level); the launches traced: 119 us -> 119 us
  no operation moved by 1% of the time
where the time goes in v4:
time: 119 us
  Pallas kernels  118 us (99%)
  local copies, waits for them, and re-layouts  1.32 us (1%)
    pallas_call x1, Pallas kernels, shards(): pl.pallas_call(kernel, out_shape=jax.ShapeDtypeStruct((2, F, rows, block)...  118 us

profile of v4, /device:TPU:1, one launch (start us, length us, event | category | flops | bytes accessed | tf_op | source)
XLA Modules:
  0.0 119.1 jit_solution(12733097530371514682)
XLA Ops:
  0.0 117.8 %interferometry.1 = bf16[2,256,16,128]{3,2,1,0:T(8,128)(2,1)S(1)} custom-call(bf16[2,128,32,128]{3,2,1,0:T(8,128)(2,1)} %x_hbm.1, s32[128,128]{1,0:T(8,128)} %mask_hbm.1, bf16[512,256]{1,0:T(8,128)(2,1)} %constant.4.clone.lag_hbm, bf16[512,256]{1,0:T(8,128)(2,1)} %constant.5.clone.tab_hbm), custom_call_target="tpu_custom_call" | custom-call | tf_op jit(solution)/shard_map/interferometry/pallas_call | solution.py:402
  117.8 1.3 %copy.6 = bf16[1,2,256,16,128]{4,3,2,1,0:T(8,128)(2,1)} copy(bf16[1,2,256,16,128]{4,3,2,1,0:T(8,128)(2,1)S(1)} %bitcast.1) | data formatting | bytes 4194304

commit v5 on v4

--- a/solution.py
+++ b/solution.py
@@ -54,7 +54,8 @@
     partner = {"tile": lax.rem(lax.axis_index("tile") + tiles // 2, tiles)}
     ahead = {"tile": lax.rem(lax.axis_index("tile") + tiles // 4, tiles)}
     behind = {"tile": lax.rem(lax.axis_index("tile") + tiles - tiles // 4, tiles)}
-    peers = [lax.rem(me + d, groups) for d in range(1, groups)]
+    order = sorted(range(1, groups), key=lambda d: abs(d - groups // 2))
+    peers = [lax.rem(me + d, groups) for d in order]
     segs, band, block = x_ref.shape[1:]
     rows = block // groups
     chunks = band // STEP

time: 119 us -> 119 us (level)
  no operation moved by 1% of the time
where the time goes in v5:
time: 119 us
  Pallas kernels  118 us (99%)
  local copies, waits for them, and re-layouts  1.32 us (1%)
    pallas_call x1, Pallas kernels, shards(): pl.pallas_call(kernel, out_shape=jax.ShapeDtypeStruct((2, F, rows, block)...  118 us

profile of v5, /device:TPU:1, one launch (start us, length us, event | category | flops | bytes accessed | tf_op | source)
XLA Modules:
  0.0 119.0 jit_solution(14594611526191319318)
XLA Ops:
  0.0 117.6 %interferometry.1 = bf16[2,256,16,128]{3,2,1,0:T(8,128)(2,1)S(1)} custom-call(bf16[2,128,32,128]{3,2,1,0:T(8,128)(2,1)} %x_hbm.1, s32[128,128]{1,0:T(8,128)} %mask_hbm.1, bf16[512,256]{1,0:T(8,128)(2,1)} %constant.4.clone.lag_hbm, bf16[512,256]{1,0:T(8,128)(2,1)} %constant.5.clone.tab_hbm), custom_call_target="tpu_custom_call" | custom-call | tf_op jit(solution)/shard_map/interferometry/pallas_call | solution.py:403
  117.6 1.3 %copy.6 = bf16[1,2,256,16,128]{4,3,2,1,0:T(8,128)(2,1)} copy(bf16[1,2,256,16,128]{4,3,2,1,0:T(8,128)(2,1)S(1)} %bitcast.1) | data formatting | bytes 4194304
